TPU v7x, 32 devices: a whole 2x2x4 slice. The times are simulated.
32 devices in a mesh: shot: 2 (over y), box: 8 (over z, x), sub: 2 (over core).
Axes of the slice: x: 2, y: 2, z: 4, core: 2. Of those that a mesh axis runs over, the one named last changes fastest.
Arguments:
- box_weights: float32 [64, 256, 128], P(('shot', 'box', 'sub')), parts along dimension 0, may hold values from -6 to 6
- velocity: float32 [8192], P('shot'), parts along dimension 0, may hold values from -4 to 4
- switch_kernel: float32 [128, 128], replicated, may hold values from -0.5 to 0.5
Outputs:
- final_weights: float32 [4, 4096, 128], P('shot', ('box', 'sub')), parts along dimension 0
There are 2 independent parts, one for each index of `shot`. A program takes and returns all parts, laid end to end along the dimension named above; an argument that names none is the same for every part. Nothing has to cross between parts.
All inputs are finite; a program needn't handle non-finite values.
Results may differ from a plain program's by a relative error of at most 0.00013.
Values sent between devices are 32-bit elements; how exact they have to be, the bound alone decides.
No kernel may reach another device: no remote copies, remote signals or barrier semaphores. Data moves between devices by JAX's collectives and lax.ppermute only.
A program may use at most 64 MiB of HBM per device.

v0:
```python
import jax
import jax.numpy as jnp
from jax import lax
from jax.sharding import PartitionSpec as P

CHEB = 8
half_root = 0.7071067811865476


def swapped(value, axis, apart):
    mask = 2**apart
    pairs = [(source, source ^ mask) for source in range(lax.axis_size(axis))]
    return lax.ppermute(value, axis, pairs)


def cheb_nodes():
    counter = jnp.arange(CHEB, dtype=jnp.float32)
    return jnp.cos(jnp.pi * (2.0 * counter + 1.0) / (2.0 * CHEB))


def lagrange_rows(points, node_values):
    differences = points[:, None] - node_values[None, :]
    node_gaps = node_values[:, None] - node_values[None, :]
    identity = jnp.eye(CHEB, dtype=jnp.float32)
    numerator = jnp.prod(
        jnp.where(identity[None, :, :] > 0.5, 1.0, differences[:, None, :]), axis=2
    )
    denominator = jnp.prod(jnp.where(identity > 0.5, 1.0, node_gaps), axis=1)
    return numerator / denominator[None, :]


def spread_coord(values, axis_dim):
    if axis_dim == 0:
        return jnp.repeat(values, CHEB)
    return jnp.tile(values, CHEB)


def level_tables(axis_dim):
    node_values = cheb_nodes()
    identity = jnp.eye(CHEB, dtype=jnp.float32)
    pair_eye = jnp.eye(2, dtype=jnp.float32)
    matrices = []
    coords = []
    for child_idx in (0, 1):
        child_pts = (node_values + (2.0 * child_idx - 1.0)) * 0.5
        lagrange = lagrange_rows(child_pts, node_values)
        if axis_dim == 0:
            single = jnp.kron(lagrange, identity)
        else:
            single = jnp.kron(identity, lagrange)
        matrices.append(jnp.kron(pair_eye, single))
        coords.append(spread_coord(child_pts, axis_dim))
    return (jnp.concatenate(matrices, 0), jnp.stack(coords), spread_coord(node_values, axis_dim))


def rotate(values, angles):
    real_part = values[..., : CHEB * CHEB]
    imag_part = values[..., CHEB * CHEB :]
    cosines = jnp.cos(angles)
    sine_vals = jnp.sin(angles)
    return jnp.concatenate(
        [real_part * cosines - imag_part * sine_vals, real_part * sine_vals + imag_part * cosines],
        -1,
    )


def merge_blocks(blocks, omegas, weights, coord_in, coord_out):
    phase = omegas[None, None, :, :, None]
    first_term = rotate(blocks[:, 0][:, :, None], -phase * coord_in[0])
    second_term = rotate(blocks[:, 1][:, :, None], -phase * coord_in[1])
    joined = jnp.concatenate([first_term, second_term], -1)
    mixture = jnp.dot(
        joined.reshape(-1, 4 * CHEB * CHEB),
        weights,
        precision=lax.Precision.HIGHEST,
        preferred_element_type=jnp.float32,
    )
    mixture = mixture.reshape(first_term.shape)
    return rotate(mixture, phase * coord_out) * half_root


def apply_switch(current, switch_kernel):
    flat = jnp.dot(
        current.reshape(-1, current.shape[-1]),
        switch_kernel,
        precision=lax.Precision.HIGHEST,
        preferred_element_type=jnp.float32,
    )
    return flat.reshape(current.shape)


def level_omegas(velocity, device, level_idx, tgt_count):
    tgt_code = device % 2 ** (level_idx + 1)
    return lax.dynamic_slice_in_dim(velocity, tgt_code * tgt_count, tgt_count)


def own_part(current, omegas, my_child, level_idx):
    vec_len = current.shape[-1]
    weights, coord_in, coord_out = level_tables(level_idx % 2)
    coord_mine = jnp.where(my_child == 0, coord_in[0], coord_in[1])
    weight_mine = jnp.where(my_child == 0, weights[:vec_len], weights[vec_len:])
    turned = rotate(current, -omegas[None, :, None] * coord_mine[None, None, :])
    return jnp.dot(
        turned.reshape(-1, vec_len),
        weight_mine,
        precision=lax.Precision.HIGHEST,
        preferred_element_type=jnp.float32,
    )


def far_part(own_term, partner, omegas, my_child, level_idx):
    vec_len = partner.shape[-1]
    weights, coord_in, coord_out = level_tables(level_idx % 2)
    coord_other = jnp.where(my_child == 0, coord_in[1], coord_in[0])
    weight_other = jnp.where(my_child == 0, weights[vec_len:], weights[:vec_len])
    turned = rotate(partner, -omegas[None, :, None] * coord_other[None, None, :])
    far_term = jnp.dot(
        turned.reshape(-1, vec_len),
        weight_other,
        precision=lax.Precision.HIGHEST,
        preferred_element_type=jnp.float32,
    )
    mixture = (own_term + far_term).reshape(partner.shape)
    return rotate(mixture, omegas[None, :, None] * coord_out[None, None, :]) * half_root


def body(box_weights, velocity, switch_kernel):
    box_count = lax.axis_size("box")
    sub_count = lax.axis_size("sub")
    box_bits = box_count.bit_length() - 1
    sub_bits = sub_count.bit_length() - 1
    levels = box_bits + sub_bits
    box_index = lax.axis_index("box")
    sub_index = lax.axis_index("sub")
    device = box_index * sub_count + sub_index
    src_count = box_weights.shape[0]
    tgt_count = box_weights.shape[1]
    vec_len = box_weights.shape[2]
    current = box_weights
    bit_idx = 0
    level_idx = bit_idx
    my_child = sub_index // 2**bit_idx % 2
    omegas = level_omegas(velocity, device, level_idx, tgt_count)
    own_term = own_part(current, omegas, my_child, level_idx)
    partner = swapped(current, "sub", bit_idx)
    current = far_part(own_term, partner, omegas, my_child, level_idx)
    spread = lax.all_to_all(current, "box", split_axis=1, concat_axis=0, tiled=True)
    block_width = tgt_count // box_count
    for bit_idx in range(box_bits):
        level_idx = sub_bits + bit_idx
        weights, coord_in, coord_out = level_tables(level_idx % 2)
        row_count = spread.shape[0]
        col_count = spread.shape[1]
        groups = 2 ** (bit_idx + 1)
        vel_table = velocity[: sub_count * groups * tgt_count].reshape(groups, sub_count, tgt_count)
        omegas = lax.dynamic_slice(
            vel_table, (0, sub_index, box_index * block_width), (groups, 1, block_width)
        )
        omegas = omegas.reshape(2, col_count)
        blocks = spread.reshape(row_count // (2 * src_count), 2, src_count, col_count, vec_len)
        merged = merge_blocks(blocks, omegas, weights, coord_in, coord_out)
        spread = merged.reshape(row_count // 2, 2 * col_count, vec_len)
        if level_idx == levels // 2 - 1:
            spread = apply_switch(spread, switch_kernel)
    current = lax.all_to_all(spread, "box", split_axis=1, concat_axis=1, tiled=True)
    return current


def solution(mesh):
    return jax.shard_map(
        body,
        mesh=mesh,
        in_specs=(P(("shot", "box", "sub"), None, None), P("shot"), P()),
        out_specs=P("shot", ("box", "sub"), None),
        check_vma=False,
    )
```

profile of v0, /device:TPU:0, one launch (start us, length us, event | category | flops | bytes accessed | tf_op | source)
XLA Modules:
  0.0 46.1 jit_solution(10633600639100690880)
XLA Ops:
  0.0 0.5 %collective-permute-start = (f32[2,256,128]{2,1,0:T(8,128)}, f32[2,256,128]{2,1,0:T(8,128)S(1)}, u32[]{:S(2)}, u32[]{:S(2)}) collective-permute-start(f32[2,256,128]{2,1,0:T(8,128)} %param.3), channel_id=1, source_target_pairs={{0,1},{1,0},{2,3},{3,2},{4,5},{5,4},{6,7},{7,6},{8,9},{9,8},{10,11... | collective-permute-start | bytes 786440 | tf_op jit(solution)/shard_map/ppermute | solution.py:13
  0.7 0.7 %copy-done.2 = f32[4096]{0:T(1024)S(1)} copy-done((f32[4096]{0:T(1024)S(1)}, f32[4096]{0:T(1024)}, u32[]{:S(2)}) %copy-start.2) | copy-done | bytes 16408
  1.8 0.2 select_reduce_fusion.2
  2.0 0.3 select_reduce_fusion.1
  2.3 0.1 broadcast_multiply_fusion
  2.5 0.1 mul.1285
  2.6 0.1 mul.1290
  2.8 0.1 mul.1344
  2.9 0.1 mul.1350
  3.2 0.5 %slice-done.1 = f32[2048]{0:T(1024)S(1)} async-done(((f32[4096]{0:T(1024)}), f32[2048]{0:T(1024)S(1)}, s32[]{:S(2)}) %slice-start.1) | async-done | bytes 8216 | tf_op jit(solution)/shard_map/slice | solution.py:155
  3.9 0.3 multiply_cosine_fusion.5
  4.2 0.3 multiply_cosine_fusion.8
  4.6 0.4 slice-done
  5.2 0.3 broadcast_select_fusion
  5.5 0.1 mul.1347
  5.7 0.1 mul.1353
  5.9 0.5 %multiply_cosine_fusion.7 = (f32[2,64,64]{2,1,0:T(8,128)S(1)}, f32[2,64,64]{2,1,0:T(8,128)S(1)}, f32[2,64,64]{2,1,0:T(8,128)S(1)}, f32[2,64,64]{2,1,0:T(8,128)S(1)}) fusion(f32[64]{0:T(128)S(1)} %squeeze_stack_reshape.16, f32[2,64]{1,0:T(2,128)S(1)} %neg.34, f32[64]{0:T(128)S(1)} %squeeze_stack_reshape.17), kind=kLoop, calls=%fused_computation.103 | loop fusion | flops 16384 | bytes 132096 | tf_op jit(solution)/shard_map/cos | solution.py:59
  6.6 1.0 %multiply_cosine_fusion.2 = (f32[256,64]{1,0:T(8,128)S(1)}, f32[256,64]{1,0:T(8,128)S(1)}, f32[256,64]{1,0:T(8,128)S(1)}, f32[256,64]{1,0:T(8,128)S(1)}) fusion(f32[64]{0:T(128)S(1)} %get-tuple-element.97, f32[256]{0:T(256)S(1)} %get-tuple-element.7, f32[64]{0:T(128)S(1)} %get-tuple-element.98), kind=kLoop, calls=%fused_computation.59 | loop fusion | flops 32768 | bytes 263680 | tf_op jit(solution)/shard_map/cos | solution.py:59
  7.6 0.2 multiply_subtract_fusion.9
  7.8 0.1 pad_maximum_fusion
  7.9 0.3 multiply_cosine_fusion.4
  8.2 0.3 multiply_cosine_fusion.11
  8.6 0.1 select_n.114
  8.7 0.1 select_n.117
  8.8 0.1 mul.1391
  8.9 0.1 mul.1392
  9.1 0.4 fusion.39
  9.5 0.2 multiply_subtract_fusion.8
  9.6 0.1 pad_maximum_fusion.1
  9.8 0.4 convolution_add_fusion
  10.1 0.1 fusion.38
  10.3 0.1 copy.42
  10.6 0.8 %copy.29 = f32[2,256,128]{2,0,1:T(2,128)} copy(f32[2,256,128]{1,2,0:T(8,128)S(1)} %maximum_multiply_fusion) | data formatting | bytes 524288 | tf_op jit(solution)/shard_map/mul | solution.py:124
  11.4 6.8 %all-to-all-start = ((f32[2,256,128]{2,0,1:T(2,128)}), f32[2,256,128]{2,0,1:T(2,128)S(1)}, u32[]{:S(2)}, u32[]{:S(2)}) async-start(f32[2,256,128]{2,0,1:T(2,128)} %copy.29), calls=%async_computation | async-start | bytes 524288 | tf_op jit(solution)/shard_map/all_to_all | solution.py:147
  18.2 0.2 multiply_cosine_fusion.9
  18.4 1.0 %multiply_cosine_fusion.1 = (f32[2,128,64]{2,1,0:T(8,128)S(1)}, f32[2,128,64]{2,1,0:T(8,128)S(1)}, f32[2,128,64]{2,1,0:T(8,128)S(1)}, f32[2,128,64]{2,1,0:T(8,128)S(1)}) fusion(f32[64]{0:T(128)S(1)} %mul.1317, f32[2,128]{1,0:T(2,128)S(1)} %neg.35, f32[64]{0:T(128)S(1)} %mul.1330), kind=kLoop, calls=%fused_computation.57 | loop fusion | flops 32768 | bytes 263680 | tf_op jit(solution)/shard_map/cos | solution.py:59
  19.4 8.4 %all-to-all-done = f32[2,256,128]{2,0,1:T(2,128)S(1)} async-done(((f32[2,256,128]{2,0,1:T(2,128)}), f32[2,256,128]{2,0,1:T(2,128)S(1)}, u32[]{:S(2)}, u32[]{:S(2)}) %all-to-all-start) | async-done | bytes 262176 | tf_op jit(solution)/shard_map/all_to_all | solution.py:147
  28.3 0.7 %fusion = f32[4,2,2,32,128]{4,3,2,1,0:T(8,128)S(1)} fusion(f32[4,2,2,32,64]{4,3,2,1,0:T(8,128)S(1)} %get-tuple-element.32, f32[4,2,2,32,64]{4,3,2,1,0:T(8,128)S(1)} %get-tuple-element.31, f32[4,2,2,32,64]{4,3,2,1,0:T(8,128)S(1)} %get-tuple-element.30, f32[4,2,2,32,64]{4,3,2,1,0:T(8,128)S(1)} %get-tuple-element.29, ...), kind=kOutput, calls=%fused_computation.2 | convolution fusion | flops 201719808 | bytes 917504 | tf_op jit(solution)/shard_map/dot_general | solution.py:72
  28.9 0.2 multiply_subtract_fusion.5
  29.1 0.4 fusion.22
  29.9 0.7 %fusion.8 = f32[2,2,2,64,128]{4,3,2,1,0:T(8,128)S(1)} fusion(f32[2,2,2,64,64]{4,3,2,1,0:T(8,128)S(1)} %get-tuple-element.24, f32[2,2,2,64,64]{4,3,2,1,0:T(8,128)S(1)} %get-tuple-element.23, f32[2,2,2,64,64]{4,3,2,1,0:T(8,128)S(1)} %get-tuple-element.22, f32[2,2,2,64,64]{4,3,2,1,0:T(8,128)S(1)} %get-tuple-element.21, f32[128,128]{1,0:T(8,128)S(1)} %mul.1392, ...), kind=kOutput, calls=%fused_computation.10 | convolution fusion | flops 201752576 | bytes 917504 | tf_op jit(solution)/shard_map/dot_general | solution.py:72
  30.6 0.2 multiply_subtract_fusion.2
  30.8 0.1 maximum_multiply_fusion.3
  31.1 0.1 multiply_subtract_fusion
  31.3 0.9 %convolution_bitcast_fusion = f32[1,2,2,128,128]{3,4,2,1,0:T(8,128)S(1)} fusion(f32[1,2,2,128,64]{4,3,2,1,0:T(8,128)S(1)} %get-tuple-element.12, f32[1,2,2,128,64]{4,3,2,1,0:T(8,128)S(1)} %get-tuple-element.11, f32[1,2,2,128,64]{4,3,2,1,0:T(8,128)S(1)} %get-tuple-element.104, f32[1,2,2,128,64]{4,3,2,1,0:T(8,128)S(1)} %get-tuple-element.105, ...), kind=kOutput, calls=%fused_computation | convolution fusion | flops 201719808 | bytes 917504 | tf_op jit(solution)/shard_map/dot_general | solution.py:72
  32.7 0.1 copy.35
  32.8 12.5 %all_to_all.20 = f32[2,256,128]{2,0,1:T(2,128)S(1)} all-to-all(f32[2,256,128]{2,0,1:T(2,128)S(1)} %copy.35), channel_id=1, replica_groups=mesh['shot'=2,'box'=8,'sub'=2] {'box'}, dimensions={1} | all-to-all | bytes 524288 | tf_op jit(solution)/shard_map/all_to_all | solution.py:165
  45.3 0.7 %copy.36 = f32[2,256,128]{2,1,0:T(8,128)} copy(f32[2,256,128]{2,0,1:T(2,128)S(1)} %all_to_all.20) | data formatting | bytes 524288 | tf_op jit(solution)/shard_map/all_to_all | solution.py:165
  (66 shorter events, 3.1 us)
Async XLA Ops:
  0.0 29.1 %copy-start = (f32[128,128]{1,0:T(8,128)S(1)}, f32[128,128]{1,0:T(8,128)}, u32[]{:S(2)}) copy-start(f32[128,128]{1,0:T(8,128)} %param.5) | copy-start | bytes 196612
  0.0 9.4 %collective-permute-start = (f32[2,256,128]{2,1,0:T(8,128)}, f32[2,256,128]{2,1,0:T(8,128)S(1)}, u32[]{:S(2)}, u32[]{:S(2)}) collective-permute-start(f32[2,256,128]{2,1,0:T(8,128)} %param.3), channel_id=1, source_target_pairs={{0,1},{1,0},{2,3},{3,2},{4,5},{5,4},{6,7},{7,6},{8,9},{9,8},{10,11... | collective-permute-start | bytes 786440 | tf_op jit(solution)/shard_map/ppermute | solution.py:13
  0.7 0.7 %copy-start.2 = (f32[4096]{0:T(1024)S(1)}, f32[4096]{0:T(1024)}, u32[]{:S(2)}) copy-start(f32[4096]{0:T(1024)} %param.4) | copy-start | bytes 49156
  3.0 0.7 %slice-start.1 = ((f32[4096]{0:T(1024)}), f32[2048]{0:T(1024)S(1)}, s32[]{:S(2)}) async-start(f32[4096]{0:T(1024)} %param.4), calls=%async_computation.3 | async-start | bytes 16384 | tf_op jit(solution)/shard_map/slice | solution.py:155
  4.2 0.7 %slice-start = ((f32[4096]{0:T(1024)}), f32[1024]{0:T(1024)S(1)}, s32[]{:S(2)}) async-start(f32[4096]{0:T(1024)} %param.4), calls=%async_computation.2 | async-start | bytes 8192 | tf_op jit(solution)/shard_map/slice | solution.py:155
  6.6 1.0 %copy-start.1 = (f32[2,256,128]{2,1,0:T(8,128)S(1)}, f32[2,256,128]{2,1,0:T(8,128)}, u32[]{:S(2)}) copy-start(f32[2,256,128]{2,1,0:T(8,128)} %param.3) | copy-start | bytes 786436
  11.4 16.4 %all-to-all-start = ((f32[2,256,128]{2,0,1:T(2,128)}), f32[2,256,128]{2,0,1:T(2,128)S(1)}, u32[]{:S(2)}, u32[]{:S(2)}) async-start(f32[2,256,128]{2,0,1:T(2,128)} %copy.29), calls=%async_computation | async-start | bytes 524288 | tf_op jit(solution)/shard_map/all_to_all | solution.py:147
where the time goes:
time: 46.4 us; the launch traced here: 46.1 us
  blocking collectives  12.5 us (27%)
  waiting for transfers between devices  8.38 us (18%)
  starting transfers between devices  7.3 us (16%)
  local copies, waits for them, and re-layouts  7.19 us (15%)
  other arithmetic  6.78 us (15%)
  matrix products  3.37 us (7%)
  between operations  0.55 us (1%)
    all_to_all x1, blocking collectives, body(): lax.all_to_all(spread, 'box', split_axis=1, concat_axis=1, tiled=True)  12.5 us
    all_to_all x1, waiting for transfers between devices, body(): lax.all_to_all(current, 'box', split_axis=1, concat_axis=0, tiled=True)  8.38 us
    all_to_all x1, starting transfers between devices, body(): lax.all_to_all(current, 'box', split_axis=1, concat_axis=0, tiled=True)  6.81 us
    cos x8, other arithmetic, rotate(): cosines = jnp.cos(angles)  3.91 us
    dot_general x3, matrix products, merge_blocks(): jnp.dot(joined.reshape(-1, 4 * CHEB * CHEB), weights, precision=lax.Preci...  2.23 us
    sub x11, other arithmetic, rotate(): real_part * cosines - imag_part * sine_vals  1.13 us
    unnamed x9, local copies, waits for them, and re-layouts  0.93 us
    slice x6, local copies, waits for them, and re-layouts, body(): velocity[:sub_count * groups * tgt_count]  0.93 us
  transfers between devices with their start and end apart: 2, of which 1 were waited for; matrix products, arithmetic and copies ran while one was open for 18% of the time, Pallas kernels for 0%

commit v1 on v0

--- a/solution.py
+++ b/solution.py
@@ -144,7 +144,18 @@
     own_term = own_part(current, omegas, my_child, level_idx)
     partner = swapped(current, "sub", bit_idx)
     current = far_part(own_term, partner, omegas, my_child, level_idx)
-    spread = lax.all_to_all(current, "box", split_axis=1, concat_axis=0, tiled=True)
+    ways, here = (lax.axis_size("box"), lax.axis_index("box"))
+    width = current.shape[1] // ways
+    shape = list(current.shape)
+    shape[1] = width
+    height = shape[0]
+    shape[0] = height * ways
+    spread = jnp.zeros(shape, current.dtype)
+    for mask_2 in range(ways):
+        part = lax.dynamic_slice_in_dim(current, (here ^ mask_2) * width, width, axis=1)
+        if mask_2:
+            part = lax.ppermute(part, "box", [(d, d ^ mask_2) for d in range(ways)])
+        spread = lax.dynamic_update_slice_in_dim(spread, part, (here ^ mask_2) * height, axis=0)
     block_width = tgt_count // box_count
     for bit_idx in range(box_bits):
         level_idx = sub_bits + bit_idx

time: 46.4 us -> 48.3 us (1.041)
  starting transfers between devices: 7.3 us -> 12.6 us
  blocking collectives: 12.5 us -> 10.6 us
  waiting for transfers between devices: 8.38 us -> 6.53 us
  other arithmetic: 6.78 us -> 7.35 us
  local copies, waits for them, and re-layouts: 7.19 us -> 6.66 us
    ppermute x0 -> x7, starting transfers between devices: none -> 12.1 us  [body(): part = lax.ppermute(part, 'box', [(d, d ^ mask_2) for d in range(ways)])]
    all_to_all x1 -> x0, waiting for transfers between devices: 8.38 us -> none  [body(): lax.all_to_all(current, 'box', split_axis=1, concat_axis=0, tiled=True)]
    all_to_all x1 -> x0, starting transfers between devices: 6.81 us -> none  [body(): lax.all_to_all(current, 'box', split_axis=1, concat_axis=0, tiled=True)]
    ppermute x0 -> x7, waiting for transfers between devices: none -> 6.52 us  [body(): part = lax.ppermute(part, 'box', [(d, d ^ mask_2) for d in range(ways)])]
    all_to_all x1, blocking collectives: 12.5 us -> 10.6 us  [body(): lax.all_to_all(spread, 'box', split_axis=1, concat_axis=1, tiled=True)]
    mul x1 -> x0, local copies, waits for them, and re-layouts: 0.84 us -> none  [far_part(): rotate(mixture, omegas[None, :, None] * coord_out[None, None, :])]
  transfers between devices with their start and end apart: 2 -> 8, of which waited for: 1 -> 3; matrix products, arithmetic and copies ran while one was open for 18% -> 18% of each run, Pallas kernels for 0% -> 0%
where the time goes in v1:
time: 48.3 us; the launch traced here: 47.8 us
  starting transfers between devices  12.6 us (26%)
  blocking collectives  10.6 us (22%)
  other arithmetic  7.35 us (15%)
  local copies, waits for them, and re-layouts  6.66 us (14%)
  waiting for transfers between devices  6.53 us (14%)
  matrix products  3.36 us (7%)
  between operations  0.65 us (1%)
    ppermute x7, starting transfers between devices, body(): part = lax.ppermute(part, 'box', [(d, d ^ mask_2) for d in range(ways)])  12.1 us
    all_to_all x1, blocking collectives, body(): lax.all_to_all(spread, 'box', split_axis=1, concat_axis=1, tiled=True)  10.6 us
    ppermute x7, waiting for transfers between devices, body(): part = lax.ppermute(part, 'box', [(d, d ^ mask_2) for d in range(ways)])  6.52 us
    cos x8, other arithmetic, rotate(): cosines = jnp.cos(angles)  4.14 us
    dot_general x3, matrix products, merge_blocks(): jnp.dot(joined.reshape(-1, 4 * CHEB * CHEB), weights, precision=lax.Preci...  2.22 us
    sub x11, other arithmetic, rotate(): real_part * cosines - imag_part * sine_vals  1.25 us
    slice x6, local copies, waits for them, and re-layouts, body(): velocity[:sub_count * groups * tgt_count]  1.24 us
    unnamed x9, local copies, waits for them, and re-layouts  1.1 us
  transfers between devices with their start and end apart: 8, of which 3 were waited for; matrix products, arithmetic and copies ran while one was open for 18% of the time, Pallas kernels for 0%

profile of v1, /device:TPU:0, one launch (start us, length us, event | category | flops | bytes accessed | tf_op | source)
XLA Modules:
  0.0 47.8 jit_solution(765300880222788616)
XLA Ops:
  0.0 0.5 %collective-permute-start = (f32[2,256,128]{2,1,0:T(8,128)}, f32[2,256,128]{2,1,0:T(8,128)S(1)}, u32[]{:S(2)}, u32[]{:S(2)}) collective-permute-start(f32[2,256,128]{2,1,0:T(8,128)} %param.3), channel_id=1, source_target_pairs={{0,1},{1,0},{2,3},{3,2},{4,5},{5,4},{6,7},{7,6},{8,9},{9,8},{10,11... | collective-permute-start | bytes 786440 | tf_op jit(solution)/shard_map/ppermute | solution.py:13
  0.7 0.7 %copy-done.2 = f32[4096]{0:T(1024)S(1)} copy-done((f32[4096]{0:T(1024)S(1)}, f32[4096]{0:T(1024)}, u32[]{:S(2)}) %copy-start.2) | copy-done | bytes 16408
  1.4 0.7 %slice-done = f32[1024]{0:T(1024)S(1)} async-done(((f32[4096]{0:T(1024)}), f32[1024]{0:T(1024)S(1)}, s32[]{:S(2)}) %slice-start) | async-done | bytes 4120 | tf_op jit(solution)/shard_map/slice | solution.py:166
  2.3 0.2 multiply_cosine_fusion.9
  2.7 0.3 multiply_cosine_fusion.5
  3.0 0.4 copy-done.3
  3.6 0.2 select_reduce_fusion.2
  3.9 0.3 select_reduce_fusion.1
  4.3 0.1 broadcast_multiply_fusion
  5.1 0.5 %slice-done.1 = f32[2048]{0:T(1024)S(1)} async-done(((f32[4096]{0:T(1024)}), f32[2048]{0:T(1024)S(1)}, s32[]{:S(2)}) %slice-start.1) | async-done | bytes 8216 | tf_op jit(solution)/shard_map/slice | solution.py:166
  5.9 0.3 multiply_cosine_fusion.6
  6.2 0.5 %multiply_cosine_fusion.2 = (f32[256,64]{1,0:T(8,128)S(1)}, f32[256,64]{1,0:T(8,128)S(1)}) fusion(f32[64]{0:T(128)S(1)} %mul.1346, f32[256]{0:T(256)S(1)} %get-tuple-element.8), kind=kLoop, calls=%fused_computation.61 | loop fusion | flops 16384 | bytes 132352 | tf_op jit(solution)/shard_map/cos | solution.py:59
  6.9 0.3 broadcast_select_fusion
  7.2 0.1 mul.1405
  7.4 0.5 %multiply_cosine_fusion.8 = (f32[2,64,64]{2,1,0:T(8,128)S(1)}, f32[2,64,64]{2,1,0:T(8,128)S(1)}, f32[2,64,64]{2,1,0:T(8,128)S(1)}, f32[2,64,64]{2,1,0:T(8,128)S(1)}) fusion(f32[64]{0:T(128)S(1)} %squeeze_stack_reshape.16, f32[2,64]{1,0:T(2,128)S(1)} %neg.34, f32[64]{0:T(128)S(1)} %squeeze_stack_reshape.17), kind=kLoop, calls=%fused_computation.105 | loop fusion | flops 16384 | bytes 132096 | tf_op jit(solution)/shard_map/cos | solution.py:59
  7.9 0.3 multiply_cosine_fusion.11
  8.2 1.0 %multiply_cosine_fusion.1 = (f32[2,128,64]{2,1,0:T(8,128)S(1)}, f32[2,128,64]{2,1,0:T(8,128)S(1)}, f32[2,128,64]{2,1,0:T(8,128)S(1)}, f32[2,128,64]{2,1,0:T(8,128)S(1)}) fusion(f32[64]{0:T(128)S(1)} %mul.1375, f32[2,128]{1,0:T(2,128)S(1)} %neg.35, f32[64]{0:T(128)S(1)} %mul.1388), kind=kLoop, calls=%fused_computation.59 | loop fusion | flops 32768 | bytes 263680 | tf_op jit(solution)/shard_map/cos | solution.py:59
  9.2 1.0 %multiply_cosine_fusion.3 = (f32[256,64]{1,0:T(8,128)S(1)}, f32[256,64]{1,0:T(8,128)S(1)}, f32[256,64]{1,0:T(8,128)S(1)}, f32[256,64]{1,0:T(8,128)S(1)}) fusion(f32[64]{0:T(128)S(1)} %get-tuple-element.103, f32[256]{0:T(256)S(1)} %get-tuple-element.7, f32[64]{0:T(128)S(1)} %get-tuple-element.104), kind=kLoop, calls=%fused_computation.63 | loop fusion | flops 32768 | bytes 263680 | tf_op jit(solution)/shard_map/cos | solution.py:59
  10.2 0.2 multiply_subtract_fusion.10
  10.4 0.1 pad_maximum_fusion
  10.6 0.1 select_n.160
  11.0 0.4 fusion.40
  11.4 0.2 multiply_subtract_fusion.9
  11.5 0.1 pad_maximum_fusion.1
  11.7 0.4 convolution_add_fusion
  12.1 0.2 multiply_subtract_fusion.8
  12.2 0.1 maximum_multiply_fusion
  12.4 2.6 %collective-permute-start.1 = (f32[2,32,128]{2,1,0:T(8,128)S(1)}, f32[2,32,128]{2,1,0:T(8,128)S(1)}, u32[]{:S(2)}, u32[]{:S(2)}) collective-permute-start(f32[2,32,128]{2,1,0:T(8,128)S(1)} %get-tuple-element.45), channel_id=1, source_target_pairs={{0,2},{2,0},{4,6},{6,4},{8,10},{10,8},{12,14},{14,12},{1,3},{3,1},... | collective-permute-start | bytes 98312 | tf_op jit(solution)/shard_map/ppermute | solution.py:157
  15.0 0.1 mul.1449
  15.3 1.6 %collective-permute-start.2 = (f32[2,32,128]{2,1,0:T(8,128)S(1)}, f32[2,32,128]{2,1,0:T(8,128)S(1)}, u32[]{:S(2)}, u32[]{:S(2)}) collective-permute-start(f32[2,32,128]{2,1,0:T(8,128)S(1)} %get-tuple-element.44), channel_id=1, source_target_pairs={{0,4},{2,6},{4,0},{6,2},{8,12},{10,14},{12,8},{14,10},{1,5},{3,7},... | collective-permute-start | bytes 98312 | tf_op jit(solution)/shard_map/ppermute | solution.py:157
  17.0 3.0 %collective-permute-start.4 = (f32[2,32,128]{2,1,0:T(8,128)S(1)}, f32[2,32,128]{2,1,0:T(8,128)S(1)}, u32[]{:S(2)}, u32[]{:S(2)}) collective-permute-start(f32[2,32,128]{2,1,0:T(8,128)S(1)} %get-tuple-element.42), channel_id=1, source_target_pairs={{0,8},{2,10},{4,12},{6,14},{8,0},{10,2},{12,4},{14,6},{1,9},{3,11}... | collective-permute-start | bytes 98312 | tf_op jit(solution)/shard_map/ppermute | solution.py:157
  19.9 1.3 %collective-permute-start.5 = (f32[2,32,128]{2,1,0:T(8,128)S(1)}, f32[2,32,128]{2,1,0:T(8,128)S(1)}, u32[]{:S(2)}, u32[]{:S(2)}) collective-permute-start(f32[2,32,128]{2,1,0:T(8,128)S(1)} %get-tuple-element.41), channel_id=1, source_target_pairs={{0,10},{2,8},{4,14},{6,12},{8,2},{10,0},{12,6},{14,4},{1,11},{3,9}... | collective-permute-start | bytes 98312 | tf_op jit(solution)/shard_map/ppermute | solution.py:157
  21.2 3.6 %collective-permute-start.6 = (f32[2,32,128]{2,1,0:T(8,128)S(1)}, f32[2,32,128]{2,1,0:T(8,128)S(1)}, u32[]{:S(2)}, u32[]{:S(2)}) collective-permute-start(f32[2,32,128]{2,1,0:T(8,128)S(1)} %get-tuple-element.40), channel_id=1, source_target_pairs={{0,12},{2,14},{4,8},{6,10},{8,4},{10,6},{12,0},{14,2},{1,13},{3,15... | collective-permute-start | bytes 98312 | tf_op jit(solution)/shard_map/ppermute | solution.py:157
  25.0 0.8 %collective-permute-done.5 = f32[2,32,128]{2,1,0:T(8,128)S(1)} collective-permute-done((f32[2,32,128]{2,1,0:T(8,128)S(1)}, f32[2,32,128]{2,1,0:T(8,128)S(1)}, u32[]{:S(2)}, u32[]{:S(2)}) %collective-permute-start.5) | collective-permute-done | bytes 32800 | tf_op jit(solution)/shard_map/ppermute | solution.py:157
  25.8 1.3 %collective-permute-done.6 = f32[2,32,128]{2,1,0:T(8,128)S(1)} collective-permute-done((f32[2,32,128]{2,1,0:T(8,128)S(1)}, f32[2,32,128]{2,1,0:T(8,128)S(1)}, u32[]{:S(2)}, u32[]{:S(2)}) %collective-permute-start.6) | collective-permute-done | bytes 32800 | tf_op jit(solution)/shard_map/ppermute | solution.py:157
  27.1 4.3 %collective-permute-done.7 = f32[2,32,128]{2,1,0:T(8,128)S(1)} collective-permute-done((f32[2,32,128]{2,1,0:T(8,128)S(1)}, f32[2,32,128]{2,1,0:T(8,128)S(1)}, u32[]{:S(2)}, u32[]{:S(2)}) %collective-permute-start.7) | collective-permute-done | bytes 32800 | tf_op jit(solution)/shard_map/ppermute | solution.py:157
  31.9 0.7 %fusion = f32[4,2,2,32,128]{4,3,2,1,0:T(8,128)S(1)} fusion(f32[4,2,2,32,64]{4,3,2,1,0:T(8,128)S(1)} %get-tuple-element.32, f32[4,2,2,32,64]{4,3,2,1,0:T(8,128)S(1)} %get-tuple-element.31, f32[4,2,2,32,64]{4,3,2,1,0:T(8,128)S(1)} %get-tuple-element.30, f32[4,2,2,32,64]{4,3,2,1,0:T(8,128)S(1)} %get-tuple-element.29, ...), kind=kOutput, calls=%fused_computation.2 | convolution fusion | flops 201719808 | bytes 917504 | tf_op jit(solution)/shard_map/dot_general | solution.py:72
  32.6 0.2 multiply_subtract_fusion.5
  32.7 0.4 fusion.22
  33.6 0.7 %fusion.8 = f32[2,2,2,64,128]{4,3,2,1,0:T(8,128)S(1)} fusion(f32[2,2,2,64,64]{4,3,2,1,0:T(8,128)S(1)} %get-tuple-element.26, f32[2,2,2,64,64]{4,3,2,1,0:T(8,128)S(1)} %get-tuple-element.25, f32[2,2,2,64,64]{4,3,2,1,0:T(8,128)S(1)} %get-tuple-element.24, f32[2,2,2,64,64]{4,3,2,1,0:T(8,128)S(1)} %get-tuple-element.23, f32[128,128]{1,0:T(8,128)S(1)} %mul.1450, ...), kind=kOutput, calls=%fused_computation.10 | convolution fusion | flops 201752576 | bytes 917504 | tf_op jit(solution)/shard_map/dot_general | solution.py:72
  34.2 0.2 multiply_subtract_fusion.2
  34.4 0.1 maximum_multiply_fusion.3
  34.8 0.1 multiply_subtract_fusion
  34.9 0.9 %convolution_bitcast_fusion = f32[1,2,2,128,128]{3,4,2,1,0:T(8,128)S(1)} fusion(f32[1,2,2,128,64]{4,3,2,1,0:T(8,128)S(1)} %get-tuple-element.12, f32[1,2,2,128,64]{4,3,2,1,0:T(8,128)S(1)} %get-tuple-element.11, f32[1,2,2,128,64]{4,3,2,1,0:T(8,128)S(1)} %get-tuple-element.110, f32[1,2,2,128,64]{4,3,2,1,0:T(8,128)S(1)} %get-tuple-element.111, ...), kind=kOutput, calls=%fused_computation | convolution fusion | flops 201719808 | bytes 917504 | tf_op jit(solution)/shard_map/dot_general | solution.py:72
  36.1 0.1 maximum_multiply_fusion.4
  36.3 0.2 copy.22
  36.5 10.6 %all_to_all.5 = f32[2,256,128]{2,0,1:T(2,128)S(1)} all-to-all(f32[2,256,128]{2,0,1:T(2,128)S(1)} %copy.22), channel_id=1, replica_groups=mesh['shot'=2,'box'=8,'sub'=2] {'box'}, dimensions={1} | all-to-all | bytes 524288 | tf_op jit(solution)/shard_map/all_to_all | solution.py:176
  47.1 0.7 %copy.23 = f32[2,256,128]{2,1,0:T(8,128)} copy(f32[2,256,128]{2,0,1:T(2,128)S(1)} %all_to_all.5) | data formatting | bytes 524288 | tf_op jit(solution)/shard_map/all_to_all | solution.py:176
  (81 shorter events, 3.8 us)
Async XLA Ops:
  0.0 32.7 %copy-start = (f32[128,128]{1,0:T(8,128)S(1)}, f32[128,128]{1,0:T(8,128)}, u32[]{:S(2)}) copy-start(f32[128,128]{1,0:T(8,128)} %param.5) | copy-start | bytes 196612
  0.0 11.4 %collective-permute-start = (f32[2,256,128]{2,1,0:T(8,128)}, f32[2,256,128]{2,1,0:T(8,128)S(1)}, u32[]{:S(2)}, u32[]{:S(2)}) collective-permute-start(f32[2,256,128]{2,1,0:T(8,128)} %param.3), channel_id=1, source_target_pairs={{0,1},{1,0},{2,3},{3,2},{4,5},{5,4},{6,7},{7,6},{8,9},{9,8},{10,11... | collective-permute-start | bytes 786440 | tf_op jit(solution)/shard_map/ppermute | solution.py:13
  0.7 0.7 %copy-start.2 = (f32[4096]{0:T(1024)S(1)}, f32[4096]{0:T(1024)}, u32[]{:S(2)}) copy-start(f32[4096]{0:T(1024)} %param.4) | copy-start | bytes 49156
  1.4 0.7 %slice-start = ((f32[4096]{0:T(1024)}), f32[1024]{0:T(1024)S(1)}, s32[]{:S(2)}) async-start(f32[4096]{0:T(1024)} %param.4), calls=%async_computation.1 | async-start | bytes 8192 | tf_op jit(solution)/shard_map/slice | solution.py:166
  2.7 0.7 %copy-start.3 = (f32[4096]{0:T(1024)S(1)}, f32[4096]{0:T(1024)}, u32[]{:S(2)}) copy-start(f32[4096]{0:T(1024)} %param.4) | copy-start | bytes 49156
  5.0 0.7 %slice-start.1 = ((f32[4096]{0:T(1024)}), f32[2048]{0:T(1024)S(1)}, s32[]{:S(2)}) async-start(f32[4096]{0:T(1024)} %param.4), calls=%async_computation.2 | async-start | bytes 16384 | tf_op jit(solution)/shard_map/slice | solution.py:166
  9.2 1.0 %copy-start.1 = (f32[2,256,128]{2,1,0:T(8,128)S(1)}, f32[2,256,128]{2,1,0:T(8,128)}, u32[]{:S(2)}) copy-start(f32[2,256,128]{2,1,0:T(8,128)} %param.3) | copy-start | bytes 786436
  12.4 8.8 %collective-permute-start.1 = (f32[2,32,128]{2,1,0:T(8,128)S(1)}, f32[2,32,128]{2,1,0:T(8,128)S(1)}, u32[]{:S(2)}, u32[]{:S(2)}) collective-permute-start(f32[2,32,128]{2,1,0:T(8,128)S(1)} %get-tuple-element.45), channel_id=1, source_target_pairs={{0,2},{2,0},{4,6},{6,4},{8,10},{10,8},{12,14},{14,12},{1,3},{3,1},... | collective-permute-start | bytes 98312 | tf_op jit(solution)/shard_map/ppermute | solution.py:157
  15.3 9.5 %collective-permute-start.2 = (f32[2,32,128]{2,1,0:T(8,128)S(1)}, f32[2,32,128]{2,1,0:T(8,128)S(1)}, u32[]{:S(2)}, u32[]{:S(2)}) collective-permute-start(f32[2,32,128]{2,1,0:T(8,128)S(1)} %get-tuple-element.44), channel_id=1, source_target_pairs={{0,4},{2,6},{4,0},{6,2},{8,12},{10,14},{12,8},{14,10},{1,5},{3,7},... | collective-permute-start | bytes 98312 | tf_op jit(solution)/shard_map/ppermute | solution.py:157
  16.9 8.0 %collective-permute-start.3 = (f32[2,32,128]{2,1,0:T(8,128)S(1)}, f32[2,32,128]{2,1,0:T(8,128)S(1)}, u32[]{:S(2)}, u32[]{:S(2)}) collective-permute-start(f32[2,32,128]{2,1,0:T(8,128)S(1)} %get-tuple-element.43), channel_id=1, source_target_pairs={{0,6},{2,4},{4,2},{6,0},{8,14},{10,12},{12,10},{14,8},{1,7},{3,5},... | collective-permute-start | bytes 98312 | tf_op jit(solution)/shard_map/ppermute | solution.py:157
  17.0 8.0 %collective-permute-start.4 = (f32[2,32,128]{2,1,0:T(8,128)S(1)}, f32[2,32,128]{2,1,0:T(8,128)S(1)}, u32[]{:S(2)}, u32[]{:S(2)}) collective-permute-start(f32[2,32,128]{2,1,0:T(8,128)S(1)} %get-tuple-element.42), channel_id=1, source_target_pairs={{0,8},{2,10},{4,12},{6,14},{8,0},{10,2},{12,4},{14,6},{1,9},{3,11}... | collective-permute-start | bytes 98312 | tf_op jit(solution)/shard_map/ppermute | solution.py:157
  19.9 5.9 %collective-permute-start.5 = (f32[2,32,128]{2,1,0:T(8,128)S(1)}, f32[2,32,128]{2,1,0:T(8,128)S(1)}, u32[]{:S(2)}, u32[]{:S(2)}) collective-permute-start(f32[2,32,128]{2,1,0:T(8,128)S(1)} %get-tuple-element.41), channel_id=1, source_target_pairs={{0,10},{2,8},{4,14},{6,12},{8,2},{10,0},{12,6},{14,4},{1,11},{3,9}... | collective-permute-start | bytes 98312 | tf_op jit(solution)/shard_map/ppermute | solution.py:157
  21.2 5.9 %collective-permute-start.6 = (f32[2,32,128]{2,1,0:T(8,128)S(1)}, f32[2,32,128]{2,1,0:T(8,128)S(1)}, u32[]{:S(2)}, u32[]{:S(2)}) collective-permute-start(f32[2,32,128]{2,1,0:T(8,128)S(1)} %get-tuple-element.40), channel_id=1, source_target_pairs={{0,12},{2,14},{4,8},{6,10},{8,4},{10,6},{12,0},{14,2},{1,13},{3,15... | collective-permute-start | bytes 98312 | tf_op jit(solution)/shard_map/ppermute | solution.py:157
  24.8 6.7 %collective-permute-start.7 = (f32[2,32,128]{2,1,0:T(8,128)S(1)}, f32[2,32,128]{2,1,0:T(8,128)S(1)}, u32[]{:S(2)}, u32[]{:S(2)}) collective-permute-start(f32[2,32,128]{2,1,0:T(8,128)S(1)} %get-tuple-element.39), channel_id=1, source_target_pairs={{0,14},{2,12},{4,10},{6,8},{8,6},{10,4},{12,2},{14,0},{1,15},{3,13... | collective-permute-start | bytes 98312 | tf_op jit(solution)/shard_map/ppermute | solution.py:157
